TPU v7x, 256 devices: a whole 4x4x8 slice. The times are simulated.
256 devices in a mesh: shard: 32 (over y, z), blk: 8 (over x, core).
Axes of the slice: x: 4, y: 4, z: 8, core: 2. Of those that a mesh axis runs over, the one named last changes fastest.
Arguments:
- request_embeddings: bfloat16 [65536, 256], P(('shard', 'blk')), may hold values from -0.5 to 0.5
- frequent_entry_matrix: bfloat16 [2048, 256], replicated, may hold values from -0.23925781 to 0.23925781
- rare_entry_matrix: float32 [65536, 256], P('shard'), may hold values from -0.24 to 0.24
- frequent_entry_lines: int32 [65536, 4], P(('shard', 'blk')), may hold values from 0 to 2047
- rare_place_parent: int32 [65536, 4], P(('shard', 'blk')), may hold values from 0 to 31, all different within a row; in each aligned block of 256 rows (0 to 255, 256 to 511, ...) at most 64 rows name the same one
- rare_local_position: int32 [65536, 4], P(('shard', 'blk')), may hold values from 0 to 2047
- rare_place_tally: int32 [65536], P(('shard', 'blk')), may hold values from 1 to 4
- sharpness_factor: float32 [1], replicated, may hold values from 4 to 16
- pairscore_additive: float32 [1], replicated, may hold values from -6 to -2
Outputs:
- request_derivative: float32 [65536, 256], P(('shard', 'blk'))
- hot_grad: float32 [2048, 256], replicated
- cold_grad: float32 [65536, 256], P(('shard', 'blk'))
Inputs may be any that keep to these rules, and one draw needn't show every extreme that they name: `rare_place_parent`: each row names 4 different owners; among the rows of one device no owner is named by more than 64 rows, a bound that some block reaches.
All inputs are finite; a program needn't handle non-finite values.
Results may differ from a plain program's by a relative error of at most 0.007.
Values may be sent and summed in bfloat16 or wider, within the bound.
No kernel may reach another device: no remote copies, remote signals or barrier semaphores. Data moves between devices by JAX's collectives and lax.ppermute only.
A program may use at most 64 MiB of HBM per device.

v0:
```python
import jax
import jax.numpy as jnp
from jax import lax
from jax.sharding import PartitionSpec as P

epsilon = 1e-06


def normalize_rows(vectors):
    radius = jnp.sqrt(jnp.sum(vectors * vectors, axis=1, keepdims=True) + epsilon)
    return (vectors / radius, radius)


def projection_backward(unit_vectors, radius, gradient):
    inner = jnp.sum(unit_vectors * gradient, axis=1, keepdims=True)
    return (gradient - unit_vectors * inner) / radius


def body(
    request_embeddings,
    frequent_entry_matrix,
    rare_entry_matrix,
    frequent_entry_lines,
    rare_place_parent,
    rare_local_position,
    rare_place_tally,
    sharpness_factor,
    pairscore_additive,
):
    pair_count, row_width = request_embeddings.shape
    owner_total = lax.axis_size("shard")
    slots_cold = rare_place_parent.shape[1]
    capacity = 2 * pair_count * slots_cold // owner_total
    sharpness_multiplier = sharpness_factor[0]
    additive_term = pairscore_additive[0]
    live_slot = jnp.arange(slots_cold)[None, :] < rare_place_tally[:, None]
    live_flat = live_slot.reshape(-1)
    owner_flat = rare_place_parent.reshape(-1)
    owner_onehot = (
        (owner_flat[:, None] == jnp.arange(owner_total)[None, :]) & live_flat[:, None]
    ).astype(jnp.int32)
    rank_before = jnp.cumsum(owner_onehot, axis=0) - owner_onehot
    position = jnp.sum(rank_before * owner_onehot, axis=1)
    dump_slot = owner_total * capacity
    bucket = jnp.where(live_flat, owner_flat * capacity + position, dump_slot)
    requests = (
        jnp.zeros((dump_slot + 1,), jnp.int32).at[bucket].set(rare_local_position.reshape(-1))
    )
    requests = requests[:dump_slot].reshape(owner_total, capacity)
    received = lax.all_to_all(requests, "shard", split_axis=0, concat_axis=0, tiled=True)
    looked = jnp.take(rare_entry_matrix, received, axis=0)
    fetched = lax.all_to_all(looked, "shard", split_axis=0, concat_axis=0, tiled=True)
    fetched_flat = fetched.reshape(dump_slot, row_width)
    picked = jnp.take(fetched_flat, jnp.minimum(bucket, dump_slot - 1), axis=0) * live_flat[
        :, None
    ].astype(jnp.float32)
    cold_sum = jnp.sum(picked.reshape(pair_count, slots_cold, row_width), axis=1)
    hot_index = jnp.arange(frequent_entry_matrix.shape[0])
    hot_counts = jnp.sum(
        (frequent_entry_lines[:, :, None] == hot_index[None, None, :]).astype(jnp.bfloat16), axis=1
    )
    hot_sum = jnp.dot(hot_counts, frequent_entry_matrix, preferred_element_type=jnp.float32)
    candidate_normalized, candidate_norm = normalize_rows(hot_sum + cold_sum)
    request_normalized, request_norm = normalize_rows(request_embeddings.astype(jnp.float32))
    candidate_reduced = candidate_normalized.astype(jnp.bfloat16)
    request_reduced = request_normalized.astype(jnp.bfloat16)
    my_base = lax.axis_index("blk") * pair_count
    target = my_base + jnp.arange(pair_count)
    block_rows = lax.all_gather(candidate_reduced, "blk", axis=0, tiled=True)
    pairwise_scores = (
        sharpness_multiplier
        * lax.dot_general(
            request_reduced,
            block_rows,
            (((1,), (1,)), ((), ())),
            preferred_element_type=jnp.float32,
        )
        + additive_term
    )
    column = jnp.arange(block_rows.shape[0])
    positive = (target[:, None] == column[None, :]).astype(jnp.float32)
    pairscore_derivative = (jax.nn.sigmoid(pairwise_scores) - positive).astype(jnp.bfloat16)
    request_running_total = jnp.dot(
        pairscore_derivative, block_rows, preferred_element_type=jnp.float32
    )
    item_acc = lax.dot_general(
        pairscore_derivative,
        request_reduced,
        (((0,), (0,)), ((), ())),
        preferred_element_type=jnp.float32,
    )
    candidate_portion = lax.psum_scatter(item_acc, "blk", scatter_dimension=0, tiled=True)
    request_derivative = projection_backward(
        request_normalized, request_norm, sharpness_multiplier * request_running_total
    )
    candidate_derivative = projection_backward(
        candidate_normalized, candidate_norm, sharpness_multiplier * candidate_portion
    ).astype(jnp.bfloat16)
    hot_local = lax.dot_general(
        hot_counts,
        candidate_derivative,
        (((0,), (0,)), ((), ())),
        preferred_element_type=jnp.float32,
    )
    slot_grads = jnp.repeat(candidate_derivative, slots_cold, axis=0)
    outgoing = jnp.zeros((dump_slot + 1, row_width), jnp.bfloat16).at[bucket].set(slot_grads)
    outgoing = outgoing[:dump_slot].reshape(owner_total, capacity, row_width)
    incoming = lax.all_to_all(outgoing, "shard", split_axis=0, concat_axis=0, tiled=True)
    cold_local = (
        jnp.zeros((rare_entry_matrix.shape[0], row_width), jnp.float32)
        .at[received.reshape(-1)]
        .add(incoming.reshape(dump_slot, row_width).astype(jnp.float32))
    )
    hot_grad = lax.psum(hot_local, ("shard", "blk"))
    cold_grad = lax.psum_scatter(cold_local, "blk", scatter_dimension=0, tiled=True)
    return (request_derivative, hot_grad, cold_grad)


def solution(mesh):
    in_specs = (
        P(("shard", "blk"), None),
        P(),
        P("shard", None),
        P(("shard", "blk"), None),
        P(("shard", "blk"), None),
        P(("shard", "blk"), None),
        P(("shard", "blk")),
        P(),
        P(),
    )
    out_specs = (P(("shard", "blk"), None), P(), P(("shard", "blk"), None))
    return jax.shard_map(body, mesh=mesh, in_specs=in_specs, out_specs=out_specs, check_vma=False)
```

profile of v0, /device:TPU:8, one launch (start us, length us, event | category | flops | bytes accessed | tf_op | source)
XLA Modules:
  0.0 536.7 jit_solution(4409312277664935398)
XLA Ops:
  11.6 9.0 %reduce-window.6 = s32[32,8,128]{2,1,0:T(8,128)S(1)} reduce-window(s32[32,8,128]{2,1,0:T(8,128)S(1)} %fusion.20, s32[]{:T(128)} %constant.23.clone.1), window={size=1x1x128 pad=0_0x0_0x127_0}, to_apply=%region_2.3 | reduce-window | flops 4161536 | bytes 262148 | tf_op jit(solution)/shard_map/reduce-window
  21.4 4.3 scatter_custom_fusion
  25.9 20.1 %all_to_all.25 = s32[32,1,64]{2,1,0:T(1,128)S(1)} all-to-all(s32[32,1,64]{2,1,0:T(1,128)S(1)} %all_to_all.16), channel_id=1, replica_groups=mesh['shard'=32,'blk'=8] {'shard'}, dimensions={0} | all-to-all | bytes 16384 | tf_op jit(solution)/shard_map/all_to_all | solution.py:50
  46.1 8.6 %gather_fusion = f32[2048,256]{1,0:T(8,128)} fusion(f32[2048,256]{1,0:T(8,128)S(1)} %copy-done, s32[2048]{0:T(1024)S(1)} %broadcast_clamp_fusion), kind=kCustom, calls=%fused_computation | custom fusion | bytes 4202496 | tf_op jit(solution)/shard_map/jit(_take)/gather | solution.py:51
  54.7 3.2 broadcast_select_fusion
  58.0 5.9 %all-to-all-start.1 = ((f32[32,64,256]{2,1,0:T(8,128)}), f32[32,64,256]{2,1,0:T(8,128)}, u32[]{:S(2)}, u32[]{:S(2)}) async-start(f32[32,64,256]{2,1,0:T(8,128)} %broadcast_select_fusion), calls=%async_computation.1 | async-start | bytes 4194304 | tf_op jit(solution)/shard_map/all_to_all | solution.py:52
  66.4 44.1 %all-to-all-done.1 = f32[32,64,256]{2,1,0:T(8,128)} async-done(((f32[32,64,256]{2,1,0:T(8,128)}), f32[32,64,256]{2,1,0:T(8,128)}, u32[]{:S(2)}, u32[]{:S(2)}) %all-to-all-start.1) | async-done | bytes 2097184 | tf_op jit(solution)/shard_map/all_to_all | solution.py:52
  110.5 6.3 %gather_fusion.1 = f32[1024,256]{1,0:T(8,128)} fusion(f32[2048,256]{1,0:T(8,128)} %bitcast.9, s32[1024]{0:T(1024)S(1)} %broadcast_clamp_fusion.1), kind=kCustom, calls=%fused_computation.1 | custom fusion | bytes 2101248 | tf_op jit(solution)/shard_map/jit(_take)/gather | solution.py:54
  116.8 2.5 gather.12
  119.3 2.5 multiply_reduce_fusion
  122.7 1.8 multiply_reduce_fusion.3
  129.0 21.9 %all-gather.2.cloned.1.call-done = bf16[2048,256]{0,1:T(8,128)(2,1)} async-done(((bf16[256,256]{0,1:T(8,128)(2,1)}), bf16[2048,256]{0,1:T(8,128)(2,1)}) %all-gather.2.cloned.1.call-update) | async-done | bytes 1048592 | tf_op jit(solution)/shard_map/all_gather | solution.py:69
  150.9 2.2 fusion.8
  155.8 37.5 %reduce-scatter.3.cloned.1.call-done = f32[256,256]{0,1:T(8,128)} async-done(((f32[2048,256]{0,1:T(8,128)}), f32[256,256]{0,1:T(8,128)}) %reduce-scatter.3.cloned.1.call-update) | async-done | bytes 262160 | tf_op jit(solution)/shard_map/reduce_scatter | solution.py:92
  197.9 2.0 reshape.299
  199.9 6.4 %scatter_custom_fusion.1 = bf16[2049,256]{1,0:T(8,128)(2,1)} fusion(s32[1024]{0:T(1024)} %bitcast.58, bf16[1024,256]{1,0:T(8,128)(2,1)} %reshape.299, bf16[]{:T(256)} %constant.21.clone.1), kind=kCustom, calls=%fused_computation.24 | custom fusion | bytes 1049600 | tf_op jit(solution)/shard_map/scatter | solution.py:106
  206.3 2.3 slice.23
  208.6 10.2 %all-to-all-start.2 = ((bf16[32,64,256]{2,1,0:T(8,128)(2,1)}), bf16[32,64,256]{2,1,0:T(8,128)(2,1)}, u32[]{:S(2)}, u32[]{:S(2)}) async-start(bf16[32,64,256]{2,1,0:T(8,128)(2,1)} %bitcast.48), calls=%async_computation.3 | async-start | bytes 2097152 | tf_op jit(solution)/shard_map/all_to_all | solution.py:108
  218.9 1.8 fusion.29
  222.1 20.6 %all-to-all-done.2 = bf16[32,64,256]{2,1,0:T(8,128)(2,1)} async-done(((bf16[32,64,256]{2,1,0:T(8,128)(2,1)}), bf16[32,64,256]{2,1,0:T(8,128)(2,1)}, u32[]{:S(2)}, u32[]{:S(2)}) %all-to-all-start.2) | async-done | bytes 1048608 | tf_op jit(solution)/shard_map/all_to_all | solution.py:108
  242.7 15.0 %scatter_custom_fusion.2 = f32[2048,256]{1,0:T(8,128)} fusion(s32[2048]{0:T(1024)S(1)} %bitcast.56, bf16[2048,256]{1,0:T(8,128)(2,1)} %bitcast.15, f32[]{:T(128)} %constant.19.clone.1), kind=kCustom, calls=%fused_computation.16 | custom fusion | flops 1048576 | bytes 3145732 | tf_op jit(solution)/shard_map/scatter-add | solution.py:112
  260.4 228.4 %all-reduce.2.cloned.1.call-done = f32[2048,256]{1,0:T(8,128)} async-done(((f32[2048,256]{1,0:T(8,128)}), f32[2048,256]{1,0:T(8,128)}) %all-reduce.2.cloned.1.call-update) | async-done | bytes 2097168 | tf_op jit(solution)/shard_map/psum | solution.py:114
  488.9 38.2 %reduce-scatter.5.cloned.1.call-done = f32[256,256]{1,0:T(8,128)} async-done(((f32[2048,256]{1,0:T(8,128)}), f32[256,256]{1,0:T(8,128)}) %reduce-scatter.5.cloned.1.call-update) | async-done | bytes 262160 | tf_op jit(solution)/shard_map/reduce_scatter | solution.py:115
  527.1 3.0 copy.95
  (92 shorter events, 23.1 us)
Async XLA Ops:
  7.2 38.9 %copy-start = (f32[2048,256]{1,0:T(8,128)S(1)}, f32[2048,256]{1,0:T(8,128)}, u32[]{:S(2)}) copy-start(f32[2048,256]{1,0:T(8,128)} %param.11) | copy-start | bytes 6291460
  7.2 13.9 %copy-start.10 = (s32[256,4]{0,1:T(4,128)S(1)}, s32[256,4]{0,1:T(4,128)}, u32[]{:S(2)}) copy-start(s32[256,4]{0,1:T(4,128)} %param.14) | copy-start | bytes 12292
  21.4 33.3 %copy-start.11 = (s32[1024,1]{0,1:T(1,128)}, s32[1024,1]{0,1:T(1,128)S(1)}, u32[]{:S(2)}) copy-start(s32[1024,1]{0,1:T(1,128)S(1)} %get-tuple-element.22) | copy-start | bytes 12292
  58.0 6.2 %copy-start.4 = (s32[256,4]{0,1:T(4,128)S(1)}, s32[256,4]{0,1:T(4,128)}, u32[]{:S(2)}) copy-start(s32[256,4]{0,1:T(4,128)} %param.13) | copy-start | bytes 12292
  58.0 6.2 %copy-start.8 = (s32[256]{0:T(256)S(1)}, s32[256]{0:T(256)}, u32[]{:S(2)}) copy-start(s32[256]{0:T(256)} %param.15) | copy-start | bytes 3076
  58.0 7.2 %copy-start.9 = (s32[256,4]{0,1:T(4,128)S(1)}, s32[256,4]{0,1:T(4,128)}, u32[]{:S(2)}) copy-start(s32[256,4]{0,1:T(4,128)} %param.12) | copy-start | bytes 12292
  58.0 52.5 %all-to-all-start.1 = ((f32[32,64,256]{2,1,0:T(8,128)}), f32[32,64,256]{2,1,0:T(8,128)}, u32[]{:S(2)}, u32[]{:S(2)}) async-start(f32[32,64,256]{2,1,0:T(8,128)} %broadcast_select_fusion), calls=%async_computation.1 | async-start | bytes 4194304 | tf_op jit(solution)/shard_map/all_to_all | solution.py:52
  63.9 87.0 %all-gather.2.cloned.1.call-start = ((), (), s32[]{:S(2)}) async-start(), calls=%async_computation.5 | async-start | bytes 1179648 | tf_op jit(solution)/shard_map/all_gather | solution.py:69
  124.5 0.9 copy-start.5
  125.2 68.1 %reduce-scatter.3.cloned.1.call-start = ((), (), s32[]{:S(2)}) async-start(), calls=%async_computation.6 | async-start | bytes 2359296 | tf_op jit(solution)/shard_map/reduce_scatter | solution.py:92
  150.9 3.2 copy-start.6
  153.0 1.0 copy-start.2
  206.3 12.6 %copy-start.1 = (bf16[256,256]{0,1:T(8,128)(2,1)S(1)}, bf16[256,256]{0,1:T(8,128)(2,1)}, u32[]{:S(2)}) copy-start(bf16[256,256]{0,1:T(8,128)(2,1)} %divide_convert_fusion) | copy-start | bytes 393220
  208.6 34.1 %all-to-all-start.2 = ((bf16[32,64,256]{2,1,0:T(8,128)(2,1)}), bf16[32,64,256]{2,1,0:T(8,128)(2,1)}, u32[]{:S(2)}, u32[]{:S(2)}) async-start(bf16[32,64,256]{2,1,0:T(8,128)(2,1)} %bitcast.48), calls=%async_computation.3 | async-start | bytes 2097152 | tf_op jit(solution)/shard_map/all_to_all | solution.py:108
  218.9 270.0 %all-reduce.2.cloned.1.call-start = ((), (), s32[]{:S(2)}) async-start(), calls=%async_computation.7 | async-start | bytes 4194304 | tf_op jit(solution)/shard_map/psum | solution.py:114
  220.8 306.4 %reduce-scatter.5.cloned.1.call-start = ((), (), s32[]{:S(2)}) async-start(), calls=%async_computation.8 | async-start | bytes 2359296 | tf_op jit(solution)/shard_map/reduce_scatter | solution.py:115
  242.7 15.1 %copy-start.3 = (bf16[256,2048]{1,0:T(8,128)(2,1)S(1)}, bf16[256,2048]{1,0:T(8,128)(2,1)}, u32[]{:S(2)}) copy-start(bf16[256,2048]{1,0:T(8,128)(2,1)} %copy-done.2) | copy-start | bytes 3145732
  242.7 15.1 %copy-start.7 = (f32[256]{0:T(256)S(1)}, f32[256]{0:T(256)}, u32[]{:S(2)}) copy-start(f32[256]{0:T(256)} %add_sqrt_fusion.1) | copy-start | bytes 3076
Sparse Core Ops, SparseCore 0:
  125.3 25.5 all-gather.1
  156.0 37.3 reduce-scatter.2
  225.6 263.2 all-reduce.1
  491.9 35.2 reduce-scatter.4
where the time goes:
time: 538 us; the launch traced here: 537 us
  waiting for transfers between devices  391 us (73%)
  local copies, waits for them, and re-layouts  46.3 us (9%)
  other arithmetic  38.2 us (7%)
  blocking collectives  20.1 us (4%)
  starting transfers between devices  16.5 us (3%)
  between operations  15.4 us (3%)
  matrix products  9.24 us (2%)
    psum x1, waiting for transfers between devices, body(): hot_grad = lax.psum(hot_local, ('shard', 'blk'))  228 us
    all_to_all x1, waiting for transfers between devices, body(): lax.all_to_all(looked, 'shard', split_axis=0, concat_axis=0, tiled=True)  44.1 us
    reduce_scatter x1, waiting for transfers between devices, body(): lax.psum_scatter(cold_local, 'blk', scatter_dimension=0, tiled=True)  38.2 us
    reduce_scatter x1, waiting for transfers between devices, body(): lax.psum_scatter(item_acc, 'blk', scatter_dimension=0, tiled=True)  37.5 us
    all_gather x1, waiting for transfers between devices, body(): block_rows = lax.all_gather(candidate_reduced, 'blk', axis=0, tiled=True)  21.9 us
    all_to_all x1, waiting for transfers between devices, body(): lax.all_to_all(outgoing, 'shard', split_axis=0, concat_axis=0, tiled=True)  20.6 us
    all_to_all x1, blocking collectives, body(): lax.all_to_all(requests, 'shard', split_axis=0, concat_axis=0, tiled=True)  20.1 us
    scatter-add x1, other arithmetic, body(): cold_local = jnp.zeros((rare_entry_matrix.shape[0], row_width), jnp.float...  15 us
  transfers between devices with their start and end apart: 6, of which 6 were waited for; matrix products, arithmetic and copies ran while one was open for 5% of the time, Pallas kernels for 0%

commit v1 on v0

--- a/solution.py
+++ b/solution.py
@@ -111,7 +111,7 @@
         .at[received.reshape(-1)]
         .add(incoming.reshape(dump_slot, row_width).astype(jnp.float32))
     )
-    hot_grad = lax.psum(hot_local, ("shard", "blk"))
+    hot_grad = lax.psum(lax.psum(hot_local, axis_name="blk"), axis_name="shard")
     cold_grad = lax.psum_scatter(cold_local, "blk", scatter_dimension=0, tiled=True)
     return (request_derivative, hot_grad, cold_grad)
 

time: 538 us -> 487 us (0.905)
  waiting for transfers between devices: 391 us -> 344 us
    psum x1 -> x2, waiting for transfers between devices: 228 us -> 170 us  [body(): hot_grad = lax.psum(lax.psum(hot_local, axis_name='blk'), axis_name='shard')]
    all_to_all x1, waiting for transfers between devices: 20.6 us -> 32.7 us  [body(): lax.all_to_all(outgoing, 'shard', split_axis=0, concat_axis=0, tiled=True)]
  transfers between devices with their start and end apart: 6 -> 7, of which waited for: 6 -> 7; matrix products, arithmetic and copies ran while one was open for 5% -> 6% of each run, Pallas kernels for 0% -> 0%
where the time goes in v1:
time: 487 us; the launch traced here: 486 us
  waiting for transfers between devices  344 us (71%)
  local copies, waits for them, and re-layouts  43.4 us (9%)
  other arithmetic  37.2 us (8%)
  blocking collectives  20.1 us (4%)
  starting transfers between devices  16.5 us (3%)
  between operations  15.4 us (3%)
  matrix products  9.24 us (2%)
    psum x2, waiting for transfers between devices, body(): hot_grad = lax.psum(lax.psum(hot_local, axis_name='blk'), axis_name='shard')  170 us
    all_to_all x1, waiting for transfers between devices, body(): lax.all_to_all(looked, 'shard', split_axis=0, concat_axis=0, tiled=True)  44.1 us
    reduce_scatter x1, waiting for transfers between devices, body(): lax.psum_scatter(cold_local, 'blk', scatter_dimension=0, tiled=True)  38 us
    reduce_scatter x1, waiting for transfers between devices, body(): lax.psum_scatter(item_acc, 'blk', scatter_dimension=0, tiled=True)  37.4 us
    all_to_all x1, waiting for transfers between devices, body(): lax.all_to_all(outgoing, 'shard', split_axis=0, concat_axis=0, tiled=True)  32.7 us
    all_gather x1, waiting for transfers between devices, body(): block_rows = lax.all_gather(candidate_reduced, 'blk', axis=0, tiled=True)  22.2 us
    all_to_all x1, blocking collectives, body(): lax.all_to_all(requests, 'shard', split_axis=0, concat_axis=0, tiled=True)  20.1 us
    scatter-add x1, other arithmetic, body(): cold_local = jnp.zeros((rare_entry_matrix.shape[0], row_width), jnp.float...  14.8 us
  transfers between devices with their start and end apart: 7, of which 7 were waited for; matrix products, arithmetic and copies ran while one was open for 6% of the time, Pallas kernels for 0%

profile of v1, /device:TPU:8, one launch (start us, length us, event | category | flops | bytes accessed | tf_op | source)
XLA Modules:
  0.0 486.0 jit_solution(14983052827430565342)
XLA Ops:
  11.6 9.0 %reduce-window.6 = s32[32,8,128]{2,1,0:T(8,128)S(1)} reduce-window(s32[32,8,128]{2,1,0:T(8,128)S(1)} %fusion.20, s32[]{:T(128)} %constant.23.clone.1), window={size=1x1x128 pad=0_0x0_0x127_0}, to_apply=%region_2.3 | reduce-window | flops 4161536 | bytes 262148 | tf_op jit(solution)/shard_map/reduce-window
  21.4 4.3 scatter_custom_fusion
  25.9 20.1 %all_to_all.25 = s32[32,1,64]{2,1,0:T(1,128)S(1)} all-to-all(s32[32,1,64]{2,1,0:T(1,128)S(1)} %all_to_all.16), channel_id=1, replica_groups=mesh['shard'=32,'blk'=8] {'shard'}, dimensions={0} | all-to-all | bytes 16384 | tf_op jit(solution)/shard_map/all_to_all | solution.py:50
  46.1 8.6 %gather_fusion = f32[2048,256]{1,0:T(8,128)} fusion(f32[2048,256]{1,0:T(8,128)S(1)} %copy-done, s32[2048]{0:T(1024)S(1)} %broadcast_clamp_fusion), kind=kCustom, calls=%fused_computation | custom fusion | bytes 4202496 | tf_op jit(solution)/shard_map/jit(_take)/gather | solution.py:51
  54.7 3.2 broadcast_select_fusion
  58.0 5.9 %all-to-all-start.1 = ((f32[32,64,256]{2,1,0:T(8,128)}), f32[32,64,256]{2,1,0:T(8,128)}, u32[]{:S(2)}, u32[]{:S(2)}) async-start(f32[32,64,256]{2,1,0:T(8,128)} %broadcast_select_fusion), calls=%async_computation.1 | async-start | bytes 4194304 | tf_op jit(solution)/shard_map/all_to_all | solution.py:52
  66.4 44.1 %all-to-all-done.1 = f32[32,64,256]{2,1,0:T(8,128)} async-done(((f32[32,64,256]{2,1,0:T(8,128)}), f32[32,64,256]{2,1,0:T(8,128)}, u32[]{:S(2)}, u32[]{:S(2)}) %all-to-all-start.1) | async-done | bytes 2097184 | tf_op jit(solution)/shard_map/all_to_all | solution.py:52
  110.5 6.3 %gather_fusion.1 = f32[1024,256]{1,0:T(8,128)} fusion(f32[2048,256]{1,0:T(8,128)} %bitcast.9, s32[1024]{0:T(1024)S(1)} %broadcast_clamp_fusion.1), kind=kCustom, calls=%fused_computation.1 | custom fusion | bytes 2101248 | tf_op jit(solution)/shard_map/jit(_take)/gather | solution.py:54
  116.8 2.5 gather.12
  119.3 2.5 multiply_reduce_fusion
  122.7 1.8 multiply_reduce_fusion.3
  128.7 22.2 %all-gather.2.cloned.1.call-done = bf16[2048,256]{0,1:T(8,128)(2,1)} async-done(((bf16[256,256]{0,1:T(8,128)(2,1)}), bf16[2048,256]{0,1:T(8,128)(2,1)}) %all-gather.2.cloned.1.call-update) | async-done | bytes 1048592 | tf_op jit(solution)/shard_map/all_gather | solution.py:69
  150.9 2.2 fusion.8
  154.1 1.8 fusion.25
  155.9 37.4 %reduce-scatter.3.cloned.1.call-done = f32[256,256]{0,1:T(8,128)} async-done(((f32[2048,256]{0,1:T(8,128)}), f32[256,256]{0,1:T(8,128)}) %reduce-scatter.3.cloned.1.call-update) | async-done | bytes 262160 | tf_op jit(solution)/shard_map/reduce_scatter | solution.py:92
  196.0 1.8 fusion.29
  198.1 69.6 %all-reduce.3.cloned.1.call-done = f32[2048,256]{1,0:T(8,128)} async-done(((f32[2048,256]{1,0:T(8,128)}), f32[2048,256]{1,0:T(8,128)}) %all-reduce.3.cloned.1.call-update) | async-done | bytes 2097168 | tf_op jit(solution)/shard_map/psum | solution.py:114
  268.8 5.6 %scatter_custom_fusion.1 = bf16[2049,256]{1,0:T(8,128)(2,1)S(1)} fusion(s32[1024]{0:T(1024)} %bitcast.59, bf16[1024,256]{1,0:T(8,128)(2,1)} %reshape.299, bf16[]{:T(256)} %constant.21.clone.1), kind=kCustom, calls=%fused_computation.24 | custom fusion | bytes 1049600 | tf_op jit(solution)/shard_map/scatter | solution.py:106
  275.5 10.2 %all-to-all-start.2 = ((bf16[32,64,256]{2,1,0:T(8,128)(2,1)}), bf16[32,64,256]{2,1,0:T(8,128)(2,1)S(1)}, u32[]{:S(2)}, u32[]{:S(2)}) async-start(bf16[32,64,256]{2,1,0:T(8,128)(2,1)} %bitcast.49), calls=%async_computation.3 | async-start | bytes 2097152 | tf_op jit(solution)/shard_map/all_to_all | solution.py:108
  287.0 32.7 %all-to-all-done.2 = bf16[32,64,256]{2,1,0:T(8,128)(2,1)S(1)} async-done(((bf16[32,64,256]{2,1,0:T(8,128)(2,1)}), bf16[32,64,256]{2,1,0:T(8,128)(2,1)S(1)}, u32[]{:S(2)}, u32[]{:S(2)}) %all-to-all-start.2) | async-done | bytes 1048608 | tf_op jit(solution)/shard_map/all_to_all | solution.py:108
  319.8 14.8 %scatter_custom_fusion.2 = f32[2048,256]{1,0:T(8,128)} fusion(s32[2048]{0:T(1024)S(1)} %bitcast.57, bf16[2048,256]{1,0:T(8,128)(2,1)S(1)} %bitcast.48, f32[]{:T(128)} %constant.19.clone.1), kind=kCustom, calls=%fused_computation.16 | custom fusion | flops 1048576 | bytes 3145732 | tf_op jit(solution)/shard_map/scatter-add | solution.py:112
  338.4 100.0 %all-reduce.5.cloned.1.call-done = f32[2048,256]{1,0:T(8,128)} async-done(((f32[2048,256]{1,0:T(8,128)}), f32[2048,256]{1,0:T(8,128)}) %all-reduce.5.cloned.1.call-update) | async-done | bytes 2097168 | tf_op jit(solution)/shard_map/psum | solution.py:114
  438.4 38.0 %reduce-scatter.5.cloned.1.call-done = f32[256,256]{1,0:T(8,128)} async-done(((f32[2048,256]{1,0:T(8,128)}), f32[256,256]{1,0:T(8,128)}) %reduce-scatter.5.cloned.1.call-update) | async-done | bytes 262160 | tf_op jit(solution)/shard_map/reduce_scatter | solution.py:115
  476.4 3.0 copy.96
  (97 shorter events, 22.8 us)
Async XLA Ops:
  7.2 38.9 %copy-start = (f32[2048,256]{1,0:T(8,128)S(1)}, f32[2048,256]{1,0:T(8,128)}, u32[]{:S(2)}) copy-start(f32[2048,256]{1,0:T(8,128)} %param.11) | copy-start | bytes 6291460
  7.2 13.9 %copy-start.11 = (s32[256,4]{0,1:T(4,128)S(1)}, s32[256,4]{0,1:T(4,128)}, u32[]{:S(2)}) copy-start(s32[256,4]{0,1:T(4,128)} %param.14) | copy-start | bytes 12292
  21.4 33.3 %copy-start.12 = (s32[1024,1]{0,1:T(1,128)}, s32[1024,1]{0,1:T(1,128)S(1)}, u32[]{:S(2)}) copy-start(s32[1024,1]{0,1:T(1,128)S(1)} %get-tuple-element.22) | copy-start | bytes 12292
  58.0 6.2 %copy-start.5 = (s32[256,4]{0,1:T(4,128)S(1)}, s32[256,4]{0,1:T(4,128)}, u32[]{:S(2)}) copy-start(s32[256,4]{0,1:T(4,128)} %param.13) | copy-start | bytes 12292
  58.0 6.2 %copy-start.9 = (s32[256]{0:T(256)S(1)}, s32[256]{0:T(256)}, u32[]{:S(2)}) copy-start(s32[256]{0:T(256)} %param.15) | copy-start | bytes 3076
  58.0 7.2 %copy-start.10 = (s32[256,4]{0,1:T(4,128)S(1)}, s32[256,4]{0,1:T(4,128)}, u32[]{:S(2)}) copy-start(s32[256,4]{0,1:T(4,128)} %param.12) | copy-start | bytes 12292
  58.0 52.5 %all-to-all-start.1 = ((f32[32,64,256]{2,1,0:T(8,128)}), f32[32,64,256]{2,1,0:T(8,128)}, u32[]{:S(2)}, u32[]{:S(2)}) async-start(f32[32,64,256]{2,1,0:T(8,128)} %broadcast_select_fusion), calls=%async_computation.1 | async-start | bytes 4194304 | tf_op jit(solution)/shard_map/all_to_all | solution.py:52
  63.9 87.0 %all-gather.2.cloned.1.call-start = ((), (), s32[]{:S(2)}) async-start(), calls=%async_computation.5 | async-start | bytes 1179648 | tf_op jit(solution)/shard_map/all_gather | solution.py:69
  124.5 0.8 copy-start.6
  125.2 68.1 %reduce-scatter.3.cloned.1.call-start = ((), (), s32[]{:S(2)}) async-start(), calls=%async_computation.6 | async-start | bytes 2359296 | tf_op jit(solution)/shard_map/reduce_scatter | solution.py:92
  150.9 3.2 copy-start.7
  153.0 1.0 copy-start.3
  155.8 111.8 %all-reduce.3.cloned.1.call-start = ((), (), s32[]{:S(2)}) async-start(), calls=%async_computation.7 | async-start | bytes 4194304 | tf_op jit(solution)/shard_map/psum | solution.py:114
  195.3 0.7 copy-start.1
  197.8 69.8 %copy-start.2 = (bf16[256,256]{0,1:T(8,128)(2,1)S(1)}, bf16[256,256]{0,1:T(8,128)(2,1)}, u32[]{:S(2)}) copy-start(bf16[256,256]{0,1:T(8,128)(2,1)} %copy-done.1) | copy-start | bytes 393220
  197.8 240.6 %all-reduce.5.cloned.1.call-start = ((), (), s32[]{:S(2)}) async-start(), calls=%async_computation.8 | async-start | bytes 4194304 | tf_op jit(solution)/shard_map/psum | solution.py:114
  275.5 44.2 %all-to-all-start.2 = ((bf16[32,64,256]{2,1,0:T(8,128)(2,1)}), bf16[32,64,256]{2,1,0:T(8,128)(2,1)S(1)}, u32[]{:S(2)}, u32[]{:S(2)}) async-start(bf16[32,64,256]{2,1,0:T(8,128)(2,1)} %bitcast.49), calls=%async_computation.3 | async-start | bytes 2097152 | tf_op jit(solution)/shard_map/all_to_all | solution.py:108
  285.7 190.7 %reduce-scatter.5.cloned.1.call-start = ((), (), s32[]{:S(2)}) async-start(), calls=%async_computation.9 | async-start | bytes 2359296 | tf_op jit(solution)/shard_map/reduce_scatter | solution.py:115
  319.8 14.8 %copy-start.8 = (f32[256]{0:T(256)S(1)}, f32[256]{0:T(256)}, u32[]{:S(2)}) copy-start(f32[256]{0:T(256)} %add_sqrt_fusion.1) | copy-start | bytes 3076
  334.6 1.2 copy-start.4
Sparse Core Ops, SparseCore 0:
  125.3 25.5 all-gather.1
  156.0 37.3 reduce-scatter.2
  198.0 69.6 all-reduce.2
  271.0 167.3 all-reduce.4
  441.4 35.0 reduce-scatter.4
